TPU v7x, 32 devices: a whole 2x2x4 slice. The times are simulated.
32 devices in a mesh: basin: 2 (over x), pair: 8 (over z, y), row: 2 (over core).
Axes of the slice: x: 2, y: 2, z: 4, core: 2. Of those that a mesh axis runs over, the one named last changes fastest.
Arguments:
- snapshots: float32 [8192, 4096], P(('basin', 'row'), 'pair'), parts along dimension 0, may hold values from -60 to 60, as said below
- plan: int32 [4, 16], replicated, may hold values from 0 to 15, as said below
Outputs:
- rotated: float32 [8192, 4096], P(('basin', 'row'), 'pair'), parts along dimension 0
There are 2 independent parts, one for each index of `basin`. A program takes and returns all parts, laid end to end along the dimension named above; an argument that names none is the same for every part. Nothing has to cross between parts.
Inputs may be any that keep to these rules, and one draw needn't show every extreme that they name: `plan`: each row of the table is a permutation of the 16 slots. Slots 2d and 2d + 1 lie on the d-th index of pair; in every round each index sends one of its two blocks to index d + 1 and the other to index d - 1 (both modulo 8). `snapshots`: real values.
All inputs are finite; a program needn't handle non-finite values.
Results may differ from a plain program's by a relative error of at most 0.0003.
Values sent between devices are 32-bit elements; how exact they have to be, the bound alone decides.
A program may use at most 64 MiB of HBM per device.

v0:
```python
import jax
import jax.numpy as jnp
from jax import lax
from jax.sharding import PartitionSpec as P

NS_ITERS = 6
epsilon = 1e-06


def from_behind(value, axis, by):
    size = lax.axis_size(axis)
    return lax.ppermute(value, axis, [(i, (i + by) % size) for i in range(size)])


def matmul(left, right):
    return jnp.dot(left, right, precision=lax.Precision.HIGHEST, preferred_element_type=jnp.float32)


def contract(left, right, left_dim, right_dim):
    return lax.dot_general(
        left,
        right,
        (((left_dim,), (right_dim,)), ((), ())),
        precision=lax.Precision.HIGHEST,
        preferred_element_type=jnp.float32,
    )


def per_device(snapshots, plan):
    width = snapshots.shape[1] // 2
    first_block = snapshots[:, :width]
    second_block = snapshots[:, width:]
    device = lax.axis_index("pair")
    pair_count = lax.axis_size("pair")
    below = (device + pair_count - 1) % pair_count
    above = (device + 1) % pair_count
    identity = jnp.eye(width, dtype=jnp.float32)
    for round_index in range(plan.shape[0]):
        joined = jnp.concatenate((first_block, second_block), axis=1)
        total = lax.psum(contract(joined, joined, 0, 0), "row")
        cross = total[:width, width:]
        diagonal = jnp.diagonal(total)
        norm_first = diagonal[:width]
        norm_second = diagonal[width:]
        coupling = cross / (norm_first[:, None] + norm_second[None, :] + epsilon)
        system = identity + contract(coupling, coupling, 1, 1)
        inverse = identity / (1.0 + jnp.sum(coupling * coupling))
        for sweep in range(NS_ITERS):
            inverse = matmul(inverse, 2.0 * identity - matmul(system, inverse))
        lifted = first_block - contract(second_block, coupling, 1, 1)
        mixed = matmul(lifted, inverse)
        new_first = 2.0 * mixed - first_block
        new_second = second_block + 2.0 * matmul(mixed, coupling)
        layout = plan[round_index]
        upper_zero = lax.dynamic_index_in_dim(layout, 2 * above, 0, False)
        upper_one = lax.dynamic_index_in_dim(layout, 2 * above + 1, 0, False)
        second_goes_up = (upper_zero == 2 * device + 1) | (upper_one == 2 * device + 1)
        going_up = jnp.where(second_goes_up, new_second, new_first)
        going_down = jnp.where(second_goes_up, new_first, new_second)
        from_below = from_behind(going_up, "pair", 1)
        from_above = from_behind(going_down, "pair", -1)
        source_zero = lax.dynamic_index_in_dim(layout, 2 * device, 0, False)
        zero_from_below = source_zero // 2 == below
        first_block = jnp.where(zero_from_below, from_below, from_above)
        second_block = jnp.where(zero_from_below, from_above, from_below)
    return jnp.concatenate((first_block, second_block), axis=1)


def solution(mesh):
    in_specs = (P(("basin", "row"), "pair"), P())
    out_specs = P(("basin", "row"), "pair")
    return jax.shard_map(
        per_device, mesh=mesh, in_specs=in_specs, out_specs=out_specs, check_vma=False
    )
```

profile of v0, /device:TPU:0, one launch (start us, length us, event | category | flops | bytes accessed | tf_op | source)
XLA Modules:
  0.0 619.5 jit_solution(1463069651718162065)
XLA Ops:
  6.5 11.1 %fusion.62 = f32[512,512]{1,0:T(8,128)} fusion(f32[2048,512]{1,0:T(8,128)} %param.2), kind=kOutput, calls=%fused_computation.145 | convolution fusion | flops 6442450944 | bytes 5242880 | tf_op jit(solution)/shard_map/dot_general | solution.py:20
  18.0 0.7 constant_dynamic-slice_fusion.2
  20.0 20.1 %all-reduce.5.cloned.1.call-done = f32[512,512]{1,0:T(8,128)} async-done(((f32[512,512]{1,0:T(8,128)}), f32[512,512]{1,0:T(8,128)}) %all-reduce.5.cloned.1.call-update) | async-done | bytes 1048592 | tf_op jit(solution)/shard_map/psum | solution.py:40
  40.1 8.6 %gather_fusion = f32[512]{0:T(512)S(1)} fusion(f32[512,512]{1,0:T(8,128)} %all-reduce.5.cloned.1.call-done, s32[512]{0:T(512)S(1)} %bitcast.122), kind=kCustom, calls=%fused_computation | custom fusion | bytes 8192 | tf_op jit(solution)/shard_map/jit(diagonal)/cond/branch_0_fun/gather | solution.py:42
  48.7 0.8 multiply_reduce_fusion.3
  50.1 0.5 convolution_add_fusion.3
  50.7 0.4 select_subtract_fusion.23
  55.3 2.1 fusion.16
  57.4 1.9 fusion.68
  59.3 3.6 broadcast_select_fusion
  62.9 1.7 collective-permute-start.1
  64.6 3.5 collective-permute-start
  70.6 84.6 %collective-permute-done.1 = f32[2048,256]{1,0:T(8,128)} collective-permute-done((f32[2048,256]{1,0:T(8,128)}, f32[2048,256]{1,0:T(8,128)}, u32[]{:S(2)}, u32[]{:S(2)}) %collective-permute-start.1) | collective-permute-done | bytes 2097184 | tf_op jit(solution)/shard_map/ppermute | solution.py:12
  155.2 2.5 collective-permute-done
  157.7 2.5 broadcast_select_fusion.2
  160.2 1.3 copy-done.5
  161.5 8.0 %fusion = f32[512,512]{1,0:T(8,128)} fusion(f32[2048,256]{1,0:T(8,128)S(1)} %get-tuple-element.20, f32[2048,256]{1,0:T(8,128)S(1)} %get-tuple-element.19), kind=kOutput, calls=%fused_computation.4 | convolution fusion | flops 6443499520 | bytes 5242880 | tf_op jit(solution)/shard_map/dot_general | solution.py:20
  171.0 17.7 %all-reduce.7.cloned.1.call-done = f32[512,512]{1,0:T(8,128)} async-done(((f32[512,512]{1,0:T(8,128)}), f32[512,512]{1,0:T(8,128)}) %all-reduce.7.cloned.1.call-update) | async-done | bytes 1048592 | tf_op jit(solution)/shard_map/psum | solution.py:40
  188.7 8.6 %gather_fusion.1 = f32[512]{0:T(512)S(1)} fusion(f32[512,512]{1,0:T(8,128)} %all-reduce.7.cloned.1.call-done, s32[512]{0:T(512)S(1)} %bitcast.123), kind=kCustom, calls=%fused_computation.1 | custom fusion | bytes 8192 | tf_op jit(solution)/shard_map/jit(diagonal)/cond/branch_0_fun/gather | solution.py:42
  197.3 0.8 multiply_reduce_fusion.2
  198.9 0.5 convolution_add_fusion.2
  199.4 0.4 select_subtract_fusion.17
  204.1 2.0 convolution_subtract_fusion.2
  206.0 1.9 fusion.74
  207.9 4.4 broadcast_select_fusion.5
  212.3 1.7 collective-permute-start.2
  214.0 3.2 collective-permute-start.3
  219.7 84.9 %collective-permute-done.2 = f32[2048,256]{1,0:T(8,128)S(1)} collective-permute-done((f32[2048,256]{1,0:T(8,128)}, f32[2048,256]{1,0:T(8,128)S(1)}, u32[]{:S(2)}, u32[]{:S(2)}) %collective-permute-start.2) | collective-permute-done | bytes 2097184 | tf_op jit(solution)/shard_map/ppermute | solution.py:12
  304.6 1.3 copy-done.11
  305.9 1.1 collective-permute-done.3
  307.0 2.5 broadcast_select_fusion.7
  309.5 1.3 copy-done.1
  310.8 8.0 %fusion.4 = f32[512,512]{1,0:T(8,128)} fusion(f32[2048,256]{1,0:T(8,128)S(1)} %get-tuple-element.18, f32[2048,256]{1,0:T(8,128)S(1)} %get-tuple-element.17), kind=kOutput, calls=%fused_computation.8 | convolution fusion | flops 6443499520 | bytes 5242880 | tf_op jit(solution)/shard_map/dot_general | solution.py:20
  318.9 0.4 all-reduce.11.cloned.1.call-start
  319.3 0.7 constant_dynamic-slice_fusion.8
  321.3 18.1 %all-reduce.9.cloned.1.call-done = f32[512,512]{1,0:T(8,128)} async-done(((f32[512,512]{1,0:T(8,128)}), f32[512,512]{1,0:T(8,128)}) %all-reduce.9.cloned.1.call-update) | async-done | bytes 1048592 | tf_op jit(solution)/shard_map/psum | solution.py:40
  339.4 8.6 %gather_fusion.2 = f32[512]{0:T(512)S(1)} fusion(f32[512,512]{1,0:T(8,128)} %all-reduce.9.cloned.1.call-done, s32[512]{0:T(512)S(1)} %bitcast.124), kind=kCustom, calls=%fused_computation.2 | custom fusion | bytes 8192 | tf_op jit(solution)/shard_map/jit(diagonal)/cond/branch_0_fun/gather | solution.py:42
  348.0 0.8 multiply_reduce_fusion.1
  349.5 0.5 convolution_add_fusion.1
  350.0 0.4 select_subtract_fusion.11
  354.7 2.0 convolution_subtract_fusion.1
  356.7 1.9 fusion.80
  358.5 4.4 broadcast_select_fusion.8
  362.9 1.7 collective-permute-start.5
  364.7 3.1 collective-permute-start.4
  370.3 84.9 %collective-permute-done.5 = f32[2048,256]{1,0:T(8,128)S(1)} collective-permute-done((f32[2048,256]{1,0:T(8,128)}, f32[2048,256]{1,0:T(8,128)S(1)}, u32[]{:S(2)}, u32[]{:S(2)}) %collective-permute-start.5) | collective-permute-done | bytes 2097184 | tf_op jit(solution)/shard_map/ppermute | solution.py:12
  455.2 1.3 copy-done.12
  456.6 1.0 collective-permute-done.4
  457.6 2.5 broadcast_select_fusion.10
  460.1 1.3 copy-done.3
  461.4 8.0 %fusion.8 = f32[512,512]{1,0:T(8,128)} fusion(f32[2048,256]{1,0:T(8,128)S(1)} %get-tuple-element.16, f32[2048,256]{1,0:T(8,128)S(1)} %get-tuple-element.15), kind=kOutput, calls=%fused_computation.12 | convolution fusion | flops 6443499520 | bytes 5242880 | tf_op jit(solution)/shard_map/dot_general | solution.py:20
  470.7 19.3 %all-reduce.11.cloned.1.call-done = f32[512,512]{1,0:T(8,128)} async-done(((f32[512,512]{1,0:T(8,128)}), f32[512,512]{1,0:T(8,128)}) %all-reduce.11.cloned.1.call-update) | async-done | bytes 1048592 | tf_op jit(solution)/shard_map/psum | solution.py:40
  490.0 8.8 %gather_fusion.3 = f32[512]{0:T(512)S(1)} fusion(f32[512,512]{1,0:T(8,128)} %all-reduce.11.cloned.1.call-done, s32[512]{0:T(512)S(1)} %bitcast.125), kind=kCustom, calls=%fused_computation.3 | custom fusion | bytes 8192 | tf_op jit(solution)/shard_map/jit(diagonal)/cond/branch_0_fun/gather | solution.py:42
  498.8 0.8 multiply_reduce_fusion
  500.3 0.5 convolution_add_fusion
  505.5 2.0 convolution_subtract_fusion
  507.5 1.9 fusion.86
  509.4 4.4 broadcast_select_fusion.13
  513.7 1.8 collective-permute-start.6
  515.5 3.0 collective-permute-start.7
  521.0 85.1 %collective-permute-done.6 = f32[2048,256]{1,0:T(8,128)S(1)} collective-permute-done((f32[2048,256]{1,0:T(8,128)}, f32[2048,256]{1,0:T(8,128)S(1)}, u32[]{:S(2)}, u32[]{:S(2)}) %collective-permute-start.6) | collective-permute-done | bytes 2097184 | tf_op jit(solution)/shard_map/ppermute | solution.py:12
  606.1 2.2 collective-permute-done.7
  608.3 1.9 broadcast_select_fusion.15
  610.1 2.5 pad_maximum_fusion
  (81 shorter events, 17.7 us)
Async XLA Ops:
  6.5 11.5 %copy-start.13 = (s32[4,16]{1,0:T(4,128)S(1)}, s32[4,16]{1,0:T(4,128)}, u32[]{:S(2)}) copy-start(s32[4,16]{1,0:T(4,128)} %param.3) | copy-start | bytes 772
  6.5 33.6 %all-reduce.5.cloned.1.call-start = ((), (), s32[]{:S(2)}) async-start(), calls=%async_computation | async-start | bytes 2097152 | tf_op jit(solution)/shard_map/psum | solution.py:40
  17.7 171.1 %all-reduce.7.cloned.1.call-start = ((), (), s32[]{:S(2)}) async-start(), calls=%async_computation.1 | async-start | bytes 2097152 | tf_op jit(solution)/shard_map/psum | solution.py:40
  40.1 8.6 %copy-start.7 = (f32[512,512]{1,0:T(8,128)S(1)}, f32[512,512]{1,0:T(8,128)}, u32[]{:S(2)}) copy-start(f32[512,512]{1,0:T(8,128)} %all-reduce.5.cloned.1.call-done) | copy-start | bytes 3145732
  53.0 2.3 copy-start
  62.9 92.3 %collective-permute-start.1 = (f32[2048,256]{1,0:T(8,128)}, f32[2048,256]{1,0:T(8,128)}, u32[]{:S(2)}, u32[]{:S(2)}) collective-permute-start(f32[2048,256]{1,0:T(8,128)} %get-tuple-element.5), channel_id=1, source_target_pairs={{0,2},{2,4},{4,6},{6,8},{8,10},{10,12},{12,14},{14,0},{1,3},{3,5},... | collective-permute-start | bytes 6291464 | tf_op jit(solution)/shard_map/ppermute | solution.py:12
  64.6 93.1 %collective-permute-start = (f32[2048,256]{1,0:T(8,128)S(1)}, f32[2048,256]{1,0:T(8,128)}, u32[]{:S(2)}, u32[]{:S(2)}) collective-permute-start(f32[2048,256]{1,0:T(8,128)S(1)} %get-tuple-element.6), channel_id=1, source_target_pairs={{0,14},{2,0},{4,2},{6,4},{8,6},{10,8},{12,10},{14,12},{1,15},{3,1}... | collective-permute-start | bytes 6291464 | tf_op jit(solution)/shard_map/ppermute | solution.py:12
  160.2 1.3 copy-start.5
  169.5 169.8 %all-reduce.9.cloned.1.call-start = ((), (), s32[]{:S(2)}) async-start(), calls=%async_computation.2 | async-start | bytes 2097152 | tf_op jit(solution)/shard_map/psum | solution.py:40
  188.7 8.6 %copy-start.10 = (f32[512,512]{1,0:T(8,128)S(1)}, f32[512,512]{1,0:T(8,128)}, u32[]{:S(2)}) copy-start(f32[512,512]{1,0:T(8,128)} %all-reduce.7.cloned.1.call-done) | copy-start | bytes 3145732
  202.1 1.9 copy-start.6
  212.3 92.3 %collective-permute-start.2 = (f32[2048,256]{1,0:T(8,128)}, f32[2048,256]{1,0:T(8,128)S(1)}, u32[]{:S(2)}, u32[]{:S(2)}) collective-permute-start(f32[2048,256]{1,0:T(8,128)} %get-tuple-element.11), channel_id=1, source_target_pairs={{0,2},{2,4},{4,6},{6,8},{8,10},{10,12},{12,14},{14,0},{1,3},{3,5},... | collective-permute-start | bytes 6291464 | tf_op jit(solution)/shard_map/ppermute | solution.py:12
  214.0 93.0 %collective-permute-start.3 = (f32[2048,256]{1,0:T(8,128)}, f32[2048,256]{1,0:T(8,128)}, u32[]{:S(2)}, u32[]{:S(2)}) collective-permute-start(f32[2048,256]{1,0:T(8,128)} %get-tuple-element.12), channel_id=1, source_target_pairs={{0,14},{2,0},{4,2},{6,4},{8,6},{10,8},{12,10},{14,12},{1,15},{3,1}... | collective-permute-start | bytes 6291464 | tf_op jit(solution)/shard_map/ppermute | solution.py:12
  304.6 1.3 copy-start.11
  309.5 1.3 copy-start.1
  318.9 171.1 %all-reduce.11.cloned.1.call-start = ((), (), s32[]{:S(2)}) async-start(), calls=%async_computation.3 | async-start | bytes 2097152 | tf_op jit(solution)/shard_map/psum | solution.py:40
  339.3 8.6 %copy-start.8 = (f32[512,512]{1,0:T(8,128)S(1)}, f32[512,512]{1,0:T(8,128)}, u32[]{:S(2)}) copy-start(f32[512,512]{1,0:T(8,128)} %all-reduce.9.cloned.1.call-done) | copy-start | bytes 3145732
  352.7 1.9 copy-start.2
  362.9 92.3 %collective-permute-start.5 = (f32[2048,256]{1,0:T(8,128)}, f32[2048,256]{1,0:T(8,128)S(1)}, u32[]{:S(2)}, u32[]{:S(2)}) collective-permute-start(f32[2048,256]{1,0:T(8,128)} %get-tuple-element.9), channel_id=1, source_target_pairs={{0,2},{2,4},{4,6},{6,8},{8,10},{10,12},{12,14},{14,0},{1,3},{3,5},... | collective-permute-start | bytes 6291464 | tf_op jit(solution)/shard_map/ppermute | solution.py:12
  364.7 92.9 %collective-permute-start.4 = (f32[2048,256]{1,0:T(8,128)}, f32[2048,256]{1,0:T(8,128)}, u32[]{:S(2)}, u32[]{:S(2)}) collective-permute-start(f32[2048,256]{1,0:T(8,128)} %get-tuple-element.10), channel_id=1, source_target_pairs={{0,14},{2,0},{4,2},{6,4},{8,6},{10,8},{12,10},{14,12},{1,15},{3,1}... | collective-permute-start | bytes 6291464 | tf_op jit(solution)/shard_map/ppermute | solution.py:12
  455.2 1.3 copy-start.12
  460.1 1.3 copy-start.3
  490.0 8.8 %copy-start.9 = (f32[512,512]{1,0:T(8,128)S(1)}, f32[512,512]{1,0:T(8,128)}, u32[]{:S(2)}) copy-start(f32[512,512]{1,0:T(8,128)} %all-reduce.11.cloned.1.call-done) | copy-start | bytes 3145732
  503.6 1.9 copy-start.4
  513.7 92.3 %collective-permute-start.6 = (f32[2048,256]{1,0:T(8,128)}, f32[2048,256]{1,0:T(8,128)S(1)}, u32[]{:S(2)}, u32[]{:S(2)}) collective-permute-start(f32[2048,256]{1,0:T(8,128)} %get-tuple-element.7), channel_id=1, source_target_pairs={{0,2},{2,4},{4,6},{6,8},{8,10},{10,12},{12,14},{14,0},{1,3},{3,5},... | collective-permute-start | bytes 6291464 | tf_op jit(solution)/shard_map/ppermute | solution.py:12
  515.5 92.8 %collective-permute-start.7 = (f32[2048,256]{1,0:T(8,128)}, f32[2048,256]{1,0:T(8,128)}, u32[]{:S(2)}, u32[]{:S(2)}) collective-permute-start(f32[2048,256]{1,0:T(8,128)} %get-tuple-element.8), channel_id=1, source_target_pairs={{0,14},{2,0},{4,2},{6,4},{8,6},{10,8},{12,10},{14,12},{1,15},{3,1}... | collective-permute-start | bytes 6291464 | tf_op jit(solution)/shard_map/ppermute | solution.py:12
Sparse Core Ops, SparseCore 0:
  17.8 22.2 all-reduce.4
  169.7 19.0 all-reduce.6
  319.0 20.3 all-reduce.8
  469.6 20.3 all-reduce.10
where the time goes:
time: 624 us; the launch traced here: 619 us
  waiting for transfers between devices  422 us (68%)
  matrix products  87.4 us (14%)
  local copies, waits for them, and re-layouts  42.5 us (7%)
  between operations  32.2 us (5%)
  starting transfers between devices  20.7 us (3%)
  other arithmetic  15.1 us (2%)
    ppermute x8, waiting for transfers between devices, from_behind(): lax.ppermute(value, axis, [(i, (i + by) % size) for i in range(size)])  346 us
    psum x4, waiting for transfers between devices, per_device(): total = lax.psum(contract(joined, joined, 0, 0), 'row')  75.2 us
    dot_general x12, matrix products, contract(): lax.dot_general(left, right, (((left_dim,), (right_dim,)), ((), ())), pre...  45.1 us
    dot_general x56, matrix products, matmul(): jnp.dot(left, right, precision=lax.Precision.HIGHEST, preferred_element_t...  42.3 us
    gather x4, local copies, waits for them, and re-layouts, per_device(): diagonal = jnp.diagonal(total)  34.5 us
    ppermute x8, starting transfers between devices, from_behind(): lax.ppermute(value, axis, [(i, (i + by) % size) for i in range(size)])  19.7 us
  transfers between devices with their start and end apart: 12, of which 12 were waited for; matrix products, arithmetic and copies ran while one was open for 0% of the time, Pallas kernels for 0%

commit v1 on v0

--- a/solution.py
+++ b/solution.py
@@ -37,7 +37,9 @@
     identity = jnp.eye(width, dtype=jnp.float32)
     for round_index in range(plan.shape[0]):
         joined = jnp.concatenate((first_block, second_block), axis=1)
-        total = lax.psum(contract(joined, joined, 0, 0), "row")
+        own = contract(joined, joined, 0, 0)
+        parts = lax.all_gather(own, "row")
+        total = jnp.sum(parts, axis=0)
         cross = total[:width, width:]
         diagonal = jnp.diagonal(total)
         norm_first = diagonal[:width]

time: 624 us -> 590 us (0.946)
  waiting for transfers between devices: 422 us -> 385 us
  local copies, waits for them, and re-layouts: 42.5 us -> 26.6 us
  matrix products: 87.4 us -> 98.4 us
  other arithmetic: 15.1 us -> 22.9 us
    psum x4 -> x0, waiting for transfers between devices: 75.2 us -> none  [per_device(): total = lax.psum(contract(joined, joined, 0, 0), 'row')]
    all_gather x0 -> x4, waiting for transfers between devices: none -> 39.2 us  [per_device(): parts = lax.all_gather(own, 'row')]
    gather x4, local copies, waits for them, and re-layouts: 34.5 us -> 18.3 us  [per_device(): diagonal = jnp.diagonal(total)]
    dot_general x12, matrix products: 45.1 us -> 56.1 us  [contract(): lax.dot_general(left, right, (((left_dim,), (right_dim,)), ((), ())), pre...]
    reduce_sum x0 -> x4, other arithmetic: none -> 7.75 us  [per_device(): total = jnp.sum(parts, axis=0)]
where the time goes in v1:
time: 590 us; the launch traced here: 586 us
  waiting for transfers between devices  385 us (65%)
  matrix products  98.4 us (17%)
  between operations  32.5 us (6%)
  local copies, waits for them, and re-layouts  26.6 us (5%)
  other arithmetic  22.9 us (4%)
  starting transfers between devices  20.8 us (4%)
    ppermute x8, waiting for transfers between devices, from_behind(): lax.ppermute(value, axis, [(i, (i + by) % size) for i in range(size)])  346 us
    dot_general x12, matrix products, contract(): lax.dot_general(left, right, (((left_dim,), (right_dim,)), ((), ())), pre...  56.1 us
    dot_general x56, matrix products, matmul(): jnp.dot(left, right, precision=lax.Precision.HIGHEST, preferred_element_t...  42.3 us
    all_gather x4, waiting for transfers between devices, per_device(): parts = lax.all_gather(own, 'row')  39.2 us
    ppermute x8, starting transfers between devices, from_behind(): lax.ppermute(value, axis, [(i, (i + by) % size) for i in range(size)])  19.8 us
    gather x4, local copies, waits for them, and re-layouts, per_device(): diagonal = jnp.diagonal(total)  18.3 us
  transfers between devices with their start and end apart: 12, of which 12 were waited for; matrix products, arithmetic and copies ran while one was open for 0% of the time, Pallas kernels for 0%

profile of v1, /device:TPU:0, one launch (start us, length us, event | category | flops | bytes accessed | tf_op | source)
XLA Modules:
  0.0 586.3 jit_solution(6188238909545415348)
XLA Ops:
  6.5 11.1 %fusion.62 = f32[512,512]{1,0:T(8,128)} fusion(f32[2048,512]{1,0:T(8,128)} %param.2), kind=kOutput, calls=%fused_computation.145 | convolution fusion | flops 6442450944 | bytes 5242880 | tf_op jit(solution)/shard_map/dot_general | solution.py:20
  18.0 0.7 constant_dynamic-slice_fusion.2
  20.1 11.0 %all-gather.9.cloned.1.call-done = f32[1024,512]{1,0:T(8,128)} async-done(((f32[512,512]{1,0:T(8,128)}), f32[1024,512]{1,0:T(8,128)}) %all-gather.9.cloned.1.call-update) | async-done | bytes 2097168 | tf_op jit(solution)/shard_map/all_gather | solution.py:41
  31.1 1.9 reduce_sum.72
  33.0 4.5 gather_fusion
  37.6 0.8 multiply_reduce_fusion.3
  38.3 0.5 convolution_add_fusion.3
  38.8 4.3 fusion.16
  48.5 1.9 fusion.68
  50.7 3.6 broadcast_select_fusion
  54.2 1.7 collective-permute-start.1
  56.0 3.5 collective-permute-start
  62.1 84.5 %collective-permute-done.1 = f32[2048,256]{1,0:T(8,128)} collective-permute-done((f32[2048,256]{1,0:T(8,128)}, f32[2048,256]{1,0:T(8,128)}, u32[]{:S(2)}, u32[]{:S(2)}) %collective-permute-start.1) | collective-permute-done | bytes 2097184 | tf_op jit(solution)/shard_map/ppermute | solution.py:12
  146.6 2.5 collective-permute-done
  149.1 2.5 broadcast_select_fusion.2
  151.6 1.3 copy-done.5
  152.9 8.0 %fusion = f32[512,512]{1,0:T(8,128)} fusion(f32[2048,256]{1,0:T(8,128)S(1)} %get-tuple-element.20, f32[2048,256]{1,0:T(8,128)S(1)} %get-tuple-element.19), kind=kOutput, calls=%fused_computation.4 | convolution fusion | flops 6443499520 | bytes 5242880 | tf_op jit(solution)/shard_map/dot_general | solution.py:20
  162.4 8.7 %all-gather.11.cloned.1.call-done = f32[1024,512]{1,0:T(8,128)} async-done(((f32[512,512]{1,0:T(8,128)}), f32[1024,512]{1,0:T(8,128)}) %all-gather.11.cloned.1.call-update) | async-done | bytes 2097168 | tf_op jit(solution)/shard_map/all_gather | solution.py:41
  171.1 1.9 reduce_sum.74
  173.1 4.5 gather_fusion.1
  177.6 0.8 multiply_reduce_fusion.2
  178.4 0.5 convolution_add_fusion.2
  178.9 4.9 convolution_subtract_fusion.2
  189.2 1.9 fusion.74
  191.1 4.4 broadcast_select_fusion.5
  195.5 1.7 collective-permute-start.2
  197.2 3.2 collective-permute-start.3
  203.1 84.7 %collective-permute-done.2 = f32[2048,256]{1,0:T(8,128)S(1)} collective-permute-done((f32[2048,256]{1,0:T(8,128)}, f32[2048,256]{1,0:T(8,128)S(1)}, u32[]{:S(2)}, u32[]{:S(2)}) %collective-permute-start.2) | collective-permute-done | bytes 2097184 | tf_op jit(solution)/shard_map/ppermute | solution.py:12
  287.8 1.3 copy-done.10
  289.1 1.1 collective-permute-done.3
  290.2 2.5 broadcast_select_fusion.7
  292.7 1.3 copy-done.1
  294.0 8.0 %fusion.4 = f32[512,512]{1,0:T(8,128)} fusion(f32[2048,256]{1,0:T(8,128)S(1)} %get-tuple-element.18, f32[2048,256]{1,0:T(8,128)S(1)} %get-tuple-element.17), kind=kOutput, calls=%fused_computation.8 | convolution fusion | flops 6443499520 | bytes 5242880 | tf_op jit(solution)/shard_map/dot_general | solution.py:20
  302.5 0.7 constant_dynamic-slice_fusion.8
  304.3 9.2 %all-gather.13.cloned.1.call-done = f32[1024,512]{1,0:T(8,128)} async-done(((f32[512,512]{1,0:T(8,128)}), f32[1024,512]{1,0:T(8,128)}) %all-gather.13.cloned.1.call-update) | async-done | bytes 2097168 | tf_op jit(solution)/shard_map/all_gather | solution.py:41
  313.6 1.9 reduce_sum.76
  315.5 4.5 gather_fusion.2
  320.1 0.8 multiply_reduce_fusion.1
  320.9 0.5 convolution_add_fusion.1
  321.4 4.9 convolution_subtract_fusion.1
  331.7 1.9 fusion.80
  333.6 4.4 broadcast_select_fusion.8
  337.9 1.7 collective-permute-start.5
  339.7 3.1 collective-permute-start.4
  345.4 84.9 %collective-permute-done.5 = f32[2048,256]{1,0:T(8,128)S(1)} collective-permute-done((f32[2048,256]{1,0:T(8,128)}, f32[2048,256]{1,0:T(8,128)S(1)}, u32[]{:S(2)}, u32[]{:S(2)}) %collective-permute-start.5) | collective-permute-done | bytes 2097184 | tf_op jit(solution)/shard_map/ppermute | solution.py:12
  430.3 1.3 copy-done.11
  431.6 1.0 collective-permute-done.4
  432.6 2.5 broadcast_select_fusion.10
  435.1 1.3 copy-done.3
  436.4 8.0 %fusion.8 = f32[512,512]{1,0:T(8,128)} fusion(f32[2048,256]{1,0:T(8,128)S(1)} %get-tuple-element.16, f32[2048,256]{1,0:T(8,128)S(1)} %get-tuple-element.15), kind=kOutput, calls=%fused_computation.12 | convolution fusion | flops 6443499520 | bytes 5242880 | tf_op jit(solution)/shard_map/dot_general | solution.py:20
  445.7 10.3 %all-gather.15.cloned.1.call-done = f32[1024,512]{1,0:T(8,128)} async-done(((f32[512,512]{1,0:T(8,128)}), f32[1024,512]{1,0:T(8,128)}) %all-gather.15.cloned.1.call-update) | async-done | bytes 2097168 | tf_op jit(solution)/shard_map/all_gather | solution.py:41
  456.0 1.9 reduce_sum.78
  458.0 4.7 gather_fusion.3
  462.7 0.8 multiply_reduce_fusion
  463.5 0.5 convolution_add_fusion
  464.1 4.9 convolution_subtract_fusion
  474.3 1.9 fusion.86
  476.2 4.4 broadcast_select_fusion.13
  480.6 1.7 collective-permute-start.6
  482.3 3.0 collective-permute-start.7
  488.0 84.9 %collective-permute-done.6 = f32[2048,256]{1,0:T(8,128)S(1)} collective-permute-done((f32[2048,256]{1,0:T(8,128)}, f32[2048,256]{1,0:T(8,128)S(1)}, u32[]{:S(2)}, u32[]{:S(2)}) %collective-permute-start.6) | collective-permute-done | bytes 2097184 | tf_op jit(solution)/shard_map/ppermute | solution.py:12
  572.9 2.2 collective-permute-done.7
  575.1 1.9 broadcast_select_fusion.15
  577.0 2.5 pad_maximum_fusion
  (83 shorter events, 19.6 us)
Async XLA Ops:
  6.5 11.5 %copy-start.12 = (s32[4,16]{1,0:T(4,128)S(1)}, s32[4,16]{1,0:T(4,128)}, u32[]{:S(2)}) copy-start(s32[4,16]{1,0:T(4,128)} %param.3) | copy-start | bytes 772
  6.5 24.5 %all-gather.9.cloned.1.call-start = ((), (), s32[]{:S(2)}) async-start(), calls=%async_computation | async-start | bytes 3145728 | tf_op jit(solution)/shard_map/all_gather | solution.py:41
  17.7 153.5 %all-gather.11.cloned.1.call-start = ((), (), s32[]{:S(2)}) async-start(), calls=%async_computation.1 | async-start | bytes 3145728 | tf_op jit(solution)/shard_map/all_gather | solution.py:41
  48.5 2.2 copy-start
  54.2 92.3 %collective-permute-start.1 = (f32[2048,256]{1,0:T(8,128)}, f32[2048,256]{1,0:T(8,128)}, u32[]{:S(2)}, u32[]{:S(2)}) collective-permute-start(f32[2048,256]{1,0:T(8,128)} %get-tuple-element.5), channel_id=1, source_target_pairs={{0,2},{2,4},{4,6},{6,8},{8,10},{10,12},{12,14},{14,0},{1,3},{3,5},... | collective-permute-start | bytes 6291464 | tf_op jit(solution)/shard_map/ppermute | solution.py:12
  56.0 93.1 %collective-permute-start = (f32[2048,256]{1,0:T(8,128)S(1)}, f32[2048,256]{1,0:T(8,128)}, u32[]{:S(2)}, u32[]{:S(2)}) collective-permute-start(f32[2048,256]{1,0:T(8,128)S(1)} %get-tuple-element.6), channel_id=1, source_target_pairs={{0,14},{2,0},{4,2},{6,4},{8,6},{10,8},{12,10},{14,12},{1,15},{3,1}... | collective-permute-start | bytes 6291464 | tf_op jit(solution)/shard_map/ppermute | solution.py:12
  151.6 1.3 copy-start.5
  161.0 152.6 %all-gather.13.cloned.1.call-start = ((), (), s32[]{:S(2)}) async-start(), calls=%async_computation.2 | async-start | bytes 3145728 | tf_op jit(solution)/shard_map/all_gather | solution.py:41
  187.3 1.9 copy-start.8
  189.2 1.9 copy-start.6
  195.5 92.3 %collective-permute-start.2 = (f32[2048,256]{1,0:T(8,128)}, f32[2048,256]{1,0:T(8,128)S(1)}, u32[]{:S(2)}, u32[]{:S(2)}) collective-permute-start(f32[2048,256]{1,0:T(8,128)} %get-tuple-element.11), channel_id=1, source_target_pairs={{0,2},{2,4},{4,6},{6,8},{8,10},{10,12},{12,14},{14,0},{1,3},{3,5},... | collective-permute-start | bytes 6291464 | tf_op jit(solution)/shard_map/ppermute | solution.py:12
  197.2 93.0 %collective-permute-start.3 = (f32[2048,256]{1,0:T(8,128)}, f32[2048,256]{1,0:T(8,128)}, u32[]{:S(2)}, u32[]{:S(2)}) collective-permute-start(f32[2048,256]{1,0:T(8,128)} %get-tuple-element.12), channel_id=1, source_target_pairs={{0,14},{2,0},{4,2},{6,4},{8,6},{10,8},{12,10},{14,12},{1,15},{3,1}... | collective-permute-start | bytes 6291464 | tf_op jit(solution)/shard_map/ppermute | solution.py:12
  287.8 1.3 copy-start.10
  292.7 1.3 copy-start.1
  302.1 153.9 %all-gather.15.cloned.1.call-start = ((), (), s32[]{:S(2)}) async-start(), calls=%async_computation.3 | async-start | bytes 3145728 | tf_op jit(solution)/shard_map/all_gather | solution.py:41
  329.7 1.9 copy-start.9
  331.7 1.9 copy-start.2
  337.9 92.3 %collective-permute-start.5 = (f32[2048,256]{1,0:T(8,128)}, f32[2048,256]{1,0:T(8,128)S(1)}, u32[]{:S(2)}, u32[]{:S(2)}) collective-permute-start(f32[2048,256]{1,0:T(8,128)} %get-tuple-element.9), channel_id=1, source_target_pairs={{0,2},{2,4},{4,6},{6,8},{8,10},{10,12},{12,14},{14,0},{1,3},{3,5},... | collective-permute-start | bytes 6291464 | tf_op jit(solution)/shard_map/ppermute | solution.py:12
  339.7 93.0 %collective-permute-start.4 = (f32[2048,256]{1,0:T(8,128)}, f32[2048,256]{1,0:T(8,128)}, u32[]{:S(2)}, u32[]{:S(2)}) collective-permute-start(f32[2048,256]{1,0:T(8,128)} %get-tuple-element.10), channel_id=1, source_target_pairs={{0,14},{2,0},{4,2},{6,4},{8,6},{10,8},{12,10},{14,12},{1,15},{3,1}... | collective-permute-start | bytes 6291464 | tf_op jit(solution)/shard_map/ppermute | solution.py:12
  430.3 1.3 copy-start.11
  435.1 1.3 copy-start.3
  472.4 1.9 copy-start.7
  474.3 1.9 copy-start.4
  480.6 92.3 %collective-permute-start.6 = (f32[2048,256]{1,0:T(8,128)}, f32[2048,256]{1,0:T(8,128)S(1)}, u32[]{:S(2)}, u32[]{:S(2)}) collective-permute-start(f32[2048,256]{1,0:T(8,128)} %get-tuple-element.7), channel_id=1, source_target_pairs={{0,2},{2,4},{4,6},{6,8},{8,10},{10,12},{12,14},{14,0},{1,3},{3,5},... | collective-permute-start | bytes 6291464 | tf_op jit(solution)/shard_map/ppermute | solution.py:12
  482.3 92.8 %collective-permute-start.7 = (f32[2048,256]{1,0:T(8,128)}, f32[2048,256]{1,0:T(8,128)}, u32[]{:S(2)}, u32[]{:S(2)}) collective-permute-start(f32[2048,256]{1,0:T(8,128)} %get-tuple-element.8), channel_id=1, source_target_pairs={{0,14},{2,0},{4,2},{6,4},{8,6},{10,8},{12,10},{14,12},{1,15},{3,1}... | collective-permute-start | bytes 6291464 | tf_op jit(solution)/shard_map/ppermute | solution.py:12
Sparse Core Ops, SparseCore 0:
  17.8 13.2 all-gather.8
  161.1 10.0 all-gather.10
  302.2 11.3 all-gather.12
  444.6 11.3 all-gather.14
